TPU v7x, 256 devices: a whole 4x4x8 slice. The times are simulated.
256 devices in a mesh: inst: 4 (over y_hi, core), elem: 64 (over x, y_lo, z).
Axes of the slice: x: 4, y: 4 (y_hi: 2, y_lo: 2; y = y_hi * 2 + y_lo), z: 8, core: 2. Of those that a mesh axis runs over, the one named last changes fastest.
Arguments:
- flow_state: float32 [8, 5, 125, 8192], P('inst', None, None, 'elem'), may hold values from -6 to 6
- flux_matrices: float32 [3, 5, 5], replicated, may hold values from -2.5 to 2.5
- derivative: float32 [3, 125, 125], replicated, may hold values from -0.5 to 0.5
- penalty: float32 [6, 5, 5], replicated, may hold values from -2.5 to 2.5
- lift_matrices: float32 [6, 125, 25], replicated, may hold values from -1.25 to 1.25
- frequency: float32 [1], replicated, may hold values from 0.5 to 2
- step_size: float32 [8192], P('elem'), may hold values from 0.05 to 0.3
- partner: int32 [8, 256], P(None, 'elem'), may hold values from 0 to 255, as said below
Outputs:
- new_state: float32 [8, 5, 125, 8192], P('inst', None, None, 'elem')
Inputs may be any that keep to these rules, and one draw needn't show every extreme that they name: For each instance t there is one whole number o_t of 0 to 63 with partner[t, p * 4 + s] = ((p + o_t) mod 64) * 4 + s for every p and s.
All inputs are finite; a program needn't handle non-finite values.
Results may differ from a plain program's by a relative error of at most 0.0003.
Values sent between devices are 32-bit elements; how exact they have to be, the bound alone decides.
A program may use at most 64 MiB of HBM per device.

v0:
```python
import math

import jax
import jax.numpy as jnp
from jax import lax
from jax.experimental import pallas as pl
from jax.experimental.pallas import tpu as pltpu
from jax.sharding import PartitionSpec as P

MESH = pl.DeviceIdType.MESH
F32 = jnp.float32
BF16 = jnp.bfloat16
HIGHEST = lax.Precision.HIGHEST

STAGES = 4
INST = 4
RING = 8
ROWS = 640
HALF = ROWS // 2
LANES = 128
STREAM = 32
FACE = 25


def split(value):
    high = value.astype(BF16)
    low = (value - high.astype(F32)).astype(BF16)
    return high, low


def kernel(
    flow_ref, flux_ref, derivative_ref, penalty_ref, lift_ref, frequency_ref, step_ref, partner_ref,
    out_ref,
    x_ref, a_send, a_recv, b_send, b_recv, base_ref, u_ref, ru_ref, wk_ref, wa_ref, wb_ref, ra_ref, rb_ref,
    sh_ref, sl_ref, r_ref, tr_send, tr_recv, t01_ref, zbuf, hbuf, dp_ref, lt_ref, pb_ref, ct_ref,
    io_sem, as_sem, ar_sem, bs_sem, br_sem, ts_sem, tr_sem, zs_sem, zr_sem, hs_sem, hr_sem, own_sem,
):
    inst = lax.axis_index("inst")
    row = lax.axis_index("elem")
    rows_total = lax.axis_size("elem")
    low = lax.rem(row, RING)
    high = lax.div(row, RING)
    north = lax.rem(row + 1, rows_total)
    south = lax.rem(row + rows_total - 1, rows_total)

    def inst_peer(distance):
        return lax.rem(inst + distance, INST)

    def low_peer(distance):
        return lax.rem(low + distance, RING)

    def high_peer(distance):
        return lax.rem(high + distance, RING)

    loads = [
        pltpu.make_async_copy(
            flow_ref.at[half, var], x_ref.at[half, pl.ds(var * 128, 125), :], io_sem.at[half * 5 + var]
        )
        for half in range(2)
        for var in range(5)
    ]
    for load in loads:
        load.start()

    tr_recv[...] = jnp.zeros_like(tr_recv)

    barrier = pltpu.get_barrier_semaphore()
    for distance in range(1, INST):
        pl.semaphore_signal(barrier, inc=1, device_id=(inst_peer(distance), row), device_id_type=MESH)
    for other in (north, south):
        pl.semaphore_signal(barrier, inc=1, device_id=(inst, other), device_id_type=MESH)
    for distance in range(1, RING):
        pl.semaphore_signal(
            barrier, inc=1, device_id=(inst, high * RING + low_peer(distance)), device_id_type=MESH
        )
        pl.semaphore_signal(
            barrier, inc=1, device_id=(inst, high_peer(distance) * RING + low), device_id_type=MESH
        )

    lane = lax.broadcasted_iota(jnp.int32, (1, LANES), 1)

    for load in loads:
        load.wait()
    for half in range(2):
        for var in range(5):
            x_ref[half, var * 128 + 125 : var * 128 + 128, :] = jnp.zeros((3, LANES), F32)
    chunk = 40

    def pack(step, carry):
        start = pl.multiple_of(step * chunk, 8)
        parts = [
            x_ref[quarter % 2, pl.ds((quarter // 2) * HALF + start, chunk), :] for quarter in range(4)
        ]
        for target in range(INST):
            packed = None
            for quarter in range(4):
                turn = (STREAM * (quarter - target)) % LANES
                moved = parts[quarter] if turn == 0 else pltpu.roll(parts[quarter], turn, 1)
                packed = moved if packed is None else jnp.where(lane >= STREAM * quarter, moved, packed)
            a_send[target, pl.ds(start, chunk), :] = packed
        return carry

    lax.fori_loop(0, HALF // chunk, pack, 0)

    pl.semaphore_wait(barrier, INST - 1 + 2 + 2 * (RING - 1))

    def exchange(send_buffer, recv_buffer, send_sem, recv_sem, distance):
        peer = inst_peer(distance)
        return pltpu.make_async_remote_copy(
            src_ref=send_buffer.at[peer],
            dst_ref=recv_buffer.at[inst],
            send_sem=send_sem.at[peer],
            recv_sem=recv_sem.at[inst],
            device_id=(peer, row),
            device_id_type=MESH,
        )

    def arrival(recv_buffer, send_buffer, send_sem, recv_sem, distance):
        peer = inst_peer(distance)
        return pltpu.make_async_remote_copy(
            src_ref=send_buffer.at[peer],
            dst_ref=recv_buffer.at[peer],
            send_sem=send_sem.at[peer],
            recv_sem=recv_sem.at[peer],
            device_id=(peer, row),
            device_id_type=MESH,
        )

    for distance in (2, 3, 1):
        exchange(a_send, a_recv, as_sem, ar_sem, distance).start()
    own = pltpu.make_async_copy(a_send.at[inst], a_recv.at[inst], own_sem)
    own.start()

    dp_ref[...] = jnp.zeros_like(dp_ref)
    for direction in range(3):
        dp_ref[direction, 0:125, 0:125] = derivative_ref[direction]

    def volume(var, carry):
        start = pl.multiple_of(var * 128, 128)
        for other in range(5):
            block = flux_ref[0, var, other] * dp_ref[0]
            block = block + flux_ref[1, var, other] * dp_ref[1]
            block = block + flux_ref[2, var, other] * dp_ref[2]
            fine, rest = split(block)
            wk_ref[pl.ds(start, 128), other * 128 : (other + 1) * 128] = fine
            wk_ref[pl.ds(start, 128), ROWS + other * 128 : ROWS + (other + 1) * 128] = fine
            wk_ref[pl.ds(start, 128), 2 * ROWS + other * 128 : 2 * ROWS + (other + 1) * 128] = rest
        return carry

    lax.fori_loop(0, 5, volume, 0)

    face_column = lax.broadcasted_iota(jnp.int32, (FACE, LANES), 1)
    face_row = lax.broadcasted_iota(jnp.int32, (FACE, LANES), 0)
    repeat = ((lax.rem(face_column, FACE) == face_row) & (face_column < 125)).astype(F32)
    var_column = lax.broadcasted_iota(jnp.int32, (5, LANES), 1)
    var_row = lax.broadcasted_iota(jnp.int32, (5, LANES), 0)
    spread = (lax.div(var_column, FACE) == var_row).astype(F32)
    lt_ref[...] = jnp.zeros_like(lt_ref)
    for face in range(6):
        lt_ref[face, 0:125, :] = jnp.dot(
            lift_ref[face], repeat, precision=HIGHEST, preferred_element_type=F32
        )
        pb_ref[face, 0:5, :] = jnp.dot(
            penalty_ref[face], spread, precision=HIGHEST, preferred_element_type=F32
        )
        target, place, width = (wb_ref, face, 256) if face < 2 else (wa_ref, face - 2, 512)
        for var in range(5):
            fine, rest = split(lt_ref[face] * pb_ref[face, var : var + 1, :])
            here = slice(var * 128, (var + 1) * 128)
            target[here, place * 128 : (place + 1) * 128] = fine
            target[here, width + place * 128 : width + (place + 1) * 128] = fine
            target[here, 2 * width + place * 128 : 2 * width + (place + 1) * 128] = rest

    to_lane = lax.broadcasted_iota(jnp.int32, (256, 256), 1)
    from_lane = lax.broadcasted_iota(jnp.int32, (256, 256), 0)
    apart = to_lane - from_lane
    turns = lax.shift_right_arithmetic(apart, 5) & 7
    aligned = (apart & 31) == 0
    spectral = jnp.zeros((256, 256), F32)
    for turn in range(1, 8):
        if turn != 4:
            weight = 0.5 * (-1) ** turn / math.tan(math.pi * turn / 8)
            spectral = jnp.where(aligned & (turns == turn), weight, spectral)
    spectral = spectral * frequency_ref[0]
    fine, rest = split(spectral)
    sh_ref[...] = fine
    sl_ref[...] = rest

    first = pltpu.roll(step_ref[...], lax.rem((INST - inst) * STREAM, LANES), 1)
    first = jnp.where(lane < STREAM, first, 0.0)
    step_lane = first + pltpu.roll(first, 32, 1) + pltpu.roll(first, 64, 1) + pltpu.roll(first, 96, 1)

    ahead = lax.shift_right_arithmetic(jnp.broadcast_to(partner_ref[:, 0:1], (8, LANES)), 2)
    behind = (2 * row + 128 - ahead) & 63

    t01_ref[...] = jnp.zeros_like(t01_ref)
    ct_ref[...] = jnp.zeros_like(ct_ref)
    tr_send[...] = jnp.zeros_like(tr_send)

    own.wait()
    for distance in (1, 2, 3):
        arrival(a_recv, a_send, as_sem, ar_sem, distance).wait_recv()

    for side in range(2):
        def unpack(step, carry, side=side):
            start = pl.multiple_of(step * chunk, 8)
            even = a_recv[2 * side, pl.ds(start, chunk), :]
            odd = a_recv[2 * side + 1, pl.ds(start, chunk), :]
            upper = jnp.where(lane < 64, even, pltpu.roll(odd, 64, 1))
            lower = jnp.where(lane < 64, pltpu.roll(even, 64, 1), odd)
            base_ref[side, pl.ds(start, chunk), :] = upper
            u_ref[side, pl.ds(start, chunk), :] = upper
            base_ref[side, pl.ds(HALF + start, chunk), :] = lower
            u_ref[side, pl.ds(HALF + start, chunk), :] = lower
            return carry

        lax.fori_loop(0, HALF // chunk, unpack, 0)

    stream = lane & 31

    def low_copy(k, distance, sender):
        return pltpu.make_async_remote_copy(
            src_ref=zbuf.at[k, sender],
            dst_ref=zbuf.at[k, sender],
            send_sem=zs_sem.at[k, distance],
            recv_sem=zr_sem.at[k, sender],
            device_id=(inst, high * RING + low_peer(distance)),
            device_id_type=MESH,
        )

    def high_copy(k, distance, sender):
        return pltpu.make_async_remote_copy(
            src_ref=hbuf.at[k, sender],
            dst_ref=hbuf.at[k, sender],
            send_sem=hs_sem.at[k, distance],
            recv_sem=hr_sem.at[k, sender],
            device_id=(inst, high_peer(distance) * RING + low),
            device_id_type=MESH,
        )

    def trace_copy(k, sent, landed, device):
        return pltpu.make_async_remote_copy(
            src_ref=tr_send.at[k, sent],
            dst_ref=tr_recv.at[k, landed],
            send_sem=ts_sem.at[k, sent],
            recv_sem=tr_sem.at[k, landed],
            device_id=device,
            device_id_type=MESH,
        )

    def northward(k):
        return trace_copy(k, 1, 0, (inst, north))

    def southward(k):
        return trace_copy(k, 0, 1, (inst, south))

    def upward(k):
        return trace_copy(k, 3, 2, (lax.rem(inst + 1, INST), row))

    def downward(k):
        return trace_copy(k, 2, 3, (lax.rem(inst + INST - 1, INST), row))

    has_above = inst < INST - 1
    has_below = inst > 0

    def stage(k, carry):
        weight = jnp.where(k == 0, 0.25, jnp.where(k == 1, 1.0 / 3.0, jnp.where(k == 2, 0.5, 1.0)))
        for side in range(2):
            for var in range(5):
                t01_ref[0, side, var * 25 : var * 25 + 25, :] = u_ref[side, var * 128 : var * 128 + 25, :]
                t01_ref[1, side, var * 25 : var * 25 + 25, :] = u_ref[
                    side, var * 128 + 100 : var * 128 + 125, :
                ]
        mixed = jnp.where(
            stream == 15,
            t01_ref[1, 0],
            jnp.where(
                stream == 16,
                t01_ref[0, 0],
                jnp.where(stream == 17, pltpu.roll(t01_ref[1, 1], 2, 1), pltpu.roll(t01_ref[0, 1], 2, 1)),
            ),
        )
        ct_ref[0] = jnp.transpose(mixed)
        zbuf[k, low, 0, 0:4, :] = ct_ref[0, pl.ds(15, 4, stride=32), :]
        zbuf[k, low, 0, 4:8, :] = ct_ref[0, pl.ds(17, 4, stride=32), :]
        zbuf[k, low, 1, 0:4, :] = ct_ref[0, pl.ds(16, 4, stride=32), :]
        zbuf[k, low, 1, 4:8, :] = ct_ref[0, pl.ds(18, 4, stride=32), :]
        for distance in (4, 3, 5, 2, 6, 1, 7):
            low_copy(k, distance, low).start()

        for side in range(2):
            for var in range(5):
                for depth in range(5):
                    tr_send[k, 0, side, pl.ds(var * 25 + depth, 5, stride=5), :] = u_ref[
                        side, pl.ds(var * 128 + depth, 5, stride=25), :
                    ]
                    tr_send[k, 1, side, pl.ds(var * 25 + depth, 5, stride=5), :] = u_ref[
                        side, pl.ds(var * 128 + 20 + depth, 5, stride=25), :
                    ]
        northward(k).start()
        southward(k).start()
        for side in range(2):
            for var in range(5):
                tr_send[k, 2, side, var * 25 : var * 25 + 25, :] = u_ref[
                    side, pl.ds(var * 128, 25, stride=5), :
                ]
                tr_send[k, 3, side, var * 25 : var * 25 + 25, :] = u_ref[
                    side, pl.ds(var * 128 + 4, 25, stride=5), :
                ]

        @pl.when(has_above)
        def _():
            upward(k).start()

        @pl.when(has_below)
        def _():
            downward(k).start()

        for side in range(2):
            here = slice(side * LANES, (side + 1) * LANES)
            fine, rest = split(u_ref[side])
            ru_ref[0:ROWS, here] = fine
            ru_ref[ROWS : 2 * ROWS, here] = rest
            ru_ref[2 * ROWS : 3 * ROWS, here] = fine
        r_ref[...] = jnp.dot(wk_ref[...], ru_ref[...], preferred_element_type=F32)
        r_ref[...] += jnp.dot(ru_ref[0:ROWS, :], sh_ref[...], preferred_element_type=F32)
        r_ref[...] += jnp.dot(ru_ref[ROWS : 2 * ROWS, :], sh_ref[...], preferred_element_type=F32)
        r_ref[...] += jnp.dot(ru_ref[0:ROWS, :], sl_ref[...], preferred_element_type=F32)

        for distance in range(1, RING):
            low_copy(k, distance, low_peer(distance)).wait_recv()
        rotor = zbuf[k, 0, 0]
        stator = zbuf[k, 0, 1]
        for other in range(1, RING):
            rotor = jnp.where((ahead & 7) == other, zbuf[k, other, 0], rotor)
            stator = jnp.where((behind & 7) == other, zbuf[k, other, 1], stator)
        hbuf[k, high, 0] = rotor
        hbuf[k, high, 1] = stator
        for distance in (3, 5, 2, 6, 1, 7, 4):
            high_copy(k, distance, high).start()

        northward(k).wait_recv()
        southward(k).wait_recv()

        @pl.when(has_below)
        def _():
            upward(k).wait_recv()

        @pl.when(has_above)
        def _():
            downward(k).wait_recv()

        for face in range(4):
            for side in range(2):
                here = slice(side * LANES, (side + 1) * LANES)
                fine, rest = split(tr_recv[k, face, side] - tr_send[k, face, side])
                ra_ref[face * 128 : (face + 1) * 128, here] = fine
                ra_ref[512 + face * 128 : 512 + (face + 1) * 128, here] = rest
                ra_ref[1024 + face * 128 : 1024 + (face + 1) * 128, here] = fine
        r_ref[...] += jnp.dot(wa_ref[...], ra_ref[...], preferred_element_type=F32)

        for distance in range(1, RING):
            high_copy(k, distance, high_peer(distance)).wait_recv()
        rotor = hbuf[k, 0, 0]
        stator = hbuf[k, 0, 1]
        for other in range(1, RING):
            rotor = jnp.where(lax.shift_right_arithmetic(ahead, 3) == other, hbuf[k, other, 0], rotor)
            stator = jnp.where(lax.shift_right_arithmetic(behind, 3) == other, hbuf[k, other, 1], stator)
        ct_ref[1, pl.ds(16, 4, stride=32), :] = rotor[0:4]
        ct_ref[1, pl.ds(14, 4, stride=32), :] = rotor[4:8]
        ct_ref[1, pl.ds(15, 4, stride=32), :] = stator[0:4]
        ct_ref[1, pl.ds(13, 4, stride=32), :] = stator[4:8]
        seen = jnp.transpose(ct_ref[1])
        for side in range(2):
            here = slice(side * LANES, (side + 1) * LANES)
            across = seen if side == 0 else pltpu.roll(seen, 2, 1)
            west = jnp.where(stream == 0, 0.0, pltpu.roll(t01_ref[1, side], 1, 1))
            west = jnp.where(stream == 16, across, west)
            east = jnp.where(stream == 31, 0.0, pltpu.roll(t01_ref[0, side], 127, 1))
            east = jnp.where(stream == 15, across, east)
            for face, value in ((0, west), (1, east)):
                fine, rest = split(value - t01_ref[face, side])
                rb_ref[face * 128 : (face + 1) * 128, here] = fine
                rb_ref[256 + face * 128 : 256 + (face + 1) * 128, here] = rest
                rb_ref[512 + face * 128 : 512 + (face + 1) * 128, here] = fine
        r_ref[...] += jnp.dot(wb_ref[...], rb_ref[...], preferred_element_type=F32)
        scale = weight * step_lane
        for side in range(2):
            u_ref[side] = base_ref[side] - scale * r_ref[:, side * LANES : (side + 1) * LANES]

        northward(k).wait_send()
        southward(k).wait_send()

        @pl.when(has_above)
        def _():
            upward(k).wait_send()

        @pl.when(has_below)
        def _():
            downward(k).wait_send()

        for distance in range(1, RING):
            low_copy(k, distance, low).wait_send()
            high_copy(k, distance, high).wait_send()
        return carry

    lax.fori_loop(0, STAGES, stage, 0)

    for target in range(INST):
        def repack(step, carry, target=target):
            start = pl.multiple_of(step * chunk, 8)
            upper = u_ref[target // 2, pl.ds(start, chunk), :]
            lower = u_ref[target // 2, pl.ds(HALF + start, chunk), :]
            if target % 2 == 0:
                packed = jnp.where(lane < 64, upper, pltpu.roll(lower, 64, 1))
            else:
                packed = jnp.where(lane < 64, pltpu.roll(upper, 64, 1), lower)
            b_send[target, pl.ds(start, chunk), :] = packed
            return carry

        lax.fori_loop(0, HALF // chunk, repack, 0)
    for distance in (2, 3, 1):
        exchange(b_send, b_recv, bs_sem, br_sem, distance).start()
    own = pltpu.make_async_copy(b_send.at[inst], b_recv.at[inst], own_sem)
    own.start()
    for distance in range(1, INST):
        exchange(a_send, a_recv, as_sem, ar_sem, distance).wait_send()
    own.wait()
    for distance in (1, 2, 3):
        arrival(b_recv, b_send, bs_sem, br_sem, distance).wait_recv()

    def deliver(step, carry):
        start = pl.multiple_of(step * chunk, 8)
        parts = [b_recv[source, pl.ds(start, chunk), :] for source in range(INST)]
        for quarter in range(4):
            whole = None
            for source in range(INST):
                turn = (STREAM * (source - quarter)) % LANES
                moved = parts[source] if turn == 0 else pltpu.roll(parts[source], turn, 1)
                whole = moved if whole is None else jnp.where(lane >= STREAM * source, moved, whole)
            x_ref[quarter % 2, pl.ds((quarter // 2) * HALF + start, chunk), :] = whole
        return carry

    lax.fori_loop(0, HALF // chunk, deliver, 0)
    stores = [
        pltpu.make_async_copy(
            x_ref.at[half, pl.ds(var * 128, 125), :], out_ref.at[half, var], io_sem.at[half * 5 + var]
        )
        for half in range(2)
        for var in range(5)
    ]
    for store in stores:
        store.start()
    for distance in range(1, INST):
        exchange(b_send, b_recv, bs_sem, br_sem, distance).wait_send()
    for store in stores:
        store.wait()


def per_device(
    flow_state, flux_matrices, derivative, penalty, lift_matrices, frequency, step_size, partner
):
    anywhere = pl.BlockSpec(memory_space=pl.ANY)
    vector = pl.BlockSpec(memory_space=pltpu.VMEM)
    scalar = pl.BlockSpec(memory_space=pltpu.SMEM)
    dma = pltpu.SemaphoreType.DMA
    return pl.pallas_call(
        kernel,
        out_shape=jax.ShapeDtypeStruct(flow_state.shape, F32),
        in_specs=[anywhere, scalar, vector, vector, vector, scalar, vector, vector],
        out_specs=anywhere,
        scratch_shapes=[
            pltpu.VMEM((2, ROWS, LANES), F32),
            pltpu.VMEM((INST, HALF, LANES), F32),
            pltpu.VMEM((INST, HALF, LANES), F32),
            pltpu.VMEM((INST, HALF, LANES), F32),
            pltpu.VMEM((INST, HALF, LANES), F32),
            pltpu.VMEM((2, ROWS, LANES), F32),
            pltpu.VMEM((2, ROWS, LANES), F32),
            pltpu.VMEM((3 * ROWS, 256), BF16),
            pltpu.VMEM((ROWS, 3 * ROWS), BF16),
            pltpu.VMEM((ROWS, 3 * 512), BF16),
            pltpu.VMEM((ROWS, 3 * 256), BF16),
            pltpu.VMEM((3 * 512, 256), BF16),
            pltpu.VMEM((3 * 256, 256), BF16),
            pltpu.VMEM((256, 256), BF16),
            pltpu.VMEM((256, 256), BF16),
            pltpu.VMEM((ROWS, 256), F32),
            pltpu.VMEM((STAGES, 4, 2, LANES, LANES), F32),
            pltpu.VMEM((STAGES, 4, 2, LANES, LANES), F32),
            pltpu.VMEM((2, 2, LANES, LANES), F32),
            pltpu.VMEM((STAGES, RING, 2, 8, LANES), F32),
            pltpu.VMEM((STAGES, RING, 2, 8, LANES), F32),
            pltpu.VMEM((3, LANES, LANES), F32),
            pltpu.VMEM((6, LANES, LANES), F32),
            pltpu.VMEM((6, 8, LANES), F32),
            pltpu.VMEM((2, LANES, LANES), F32),
            dma((10,)),
            dma((INST,)),
            dma((INST,)),
            dma((INST,)),
            dma((INST,)),
            dma((STAGES, 4)),
            dma((STAGES, 4)),
            dma((STAGES, RING)),
            dma((STAGES, RING)),
            dma((STAGES, RING)),
            dma((STAGES, RING)),
            dma,
        ],
        compiler_params=pltpu.CompilerParams(
            collective_id=0, has_side_effects=True, vmem_limit_bytes=48 * 1024 * 1024
        ),
    )(
        flow_state, flux_matrices, derivative, penalty, lift_matrices, frequency,
        step_size.reshape(1, LANES), partner,
    )


def solution(mesh):
    placed = (P("inst", None, None, "elem"), P(), P(), P(), P(), P(), P("elem"), P(None, "elem"))
    return jax.shard_map(
        per_device,
        mesh=mesh,
        in_specs=placed,
        out_specs=P("inst", None, None, "elem"),
        check_vma=False,
    )
```

profile of v0, /device:TPU:1, one launch (start us, length us, event | category | flops | bytes accessed | tf_op | source)
XLA Modules:
  0.0 78.6 jit_solution(17684552639054527457)
XLA Ops:
  0.0 0.0 copy-start.3
  0.0 0.0 copy-start.2
  0.7 0.0 copy-done.3
  0.7 0.1 copy.13.partner_ref
  0.8 0.7 copy.10.flux_ref
  1.5 0.0 copy-done.2
  1.5 1.1 %copy.12.lift_ref = f32[6,125,25]{2,1,0:T(8,128)S(1)} copy(f32[6,125,25]{1,2,0:T(8,128)} %param.12) | data formatting | bytes 150000 | tf_op args[4]
  2.6 0.0 copy-start
  2.6 0.0 copy-start.1
  2.6 1.2 %copy.9.flow_ref = f32[2,5,125,128]{3,2,1,0:T(8,128)S(1)} copy(f32[2,5,125,128]{3,0,2,1:T(2,128)} %param.8) | data formatting | bytes 1280000 | tf_op args[0]
  3.8 0.0 copy-done
  3.8 0.0 copy-done.1
  3.8 73.4 %shard_map.82 = f32[2,5,125,128]{3,2,1,0:T(8,128)S(1)} custom-call(f32[2,5,125,128]{3,2,1,0:T(8,128)S(1)} %copy.9.flow_ref, f32[3,5,5]{2,1,0:T(8,128)S(1)} %copy.10.flux_ref, f32[3,125,125]{2,1,0:T(8,128)S(1)} %copy-done, f32[6,5,5]{2,1,0:T(8,128)S(1)} %copy.11.penalty_ref, f32[6,125,25]{2,1,0:T(8,128)S(1)} %copy.12.lift_ref, f32[1]{0:T(128)S(6)} %copy.15.frequency_ref, ...), custom_call_target="tpu_custom_call" | custom-call | tf_op jit(solution)/shard_map/pallas_call | solution.py:467
  77.2 1.3 %copy.14 = f32[2,5,125,128]{3,0,2,1:T(2,128)} copy(f32[2,5,125,128]{3,2,1,0:T(8,128)S(1)} %shard_map.82) | data formatting | bytes 1280000 | tf_op jit(solution)/shard_map/pallas_call | solution.py:467
  (1 shorter events, 0.0 us)
Async XLA Ops:
  0.0 0.7 copy-start.3
  0.0 1.5 %copy-start.2 = (f32[6,5,5]{2,0,1:T(8,128)S(1)}, f32[6,5,5]{2,0,1:T(8,128)}, u32[]{:S(2)}) copy-start(f32[6,5,5]{2,0,1:T(8,128)} %param.11) | copy-start | bytes 1804
  2.6 1.2 %copy-start = (f32[3,125,125]{2,1,0:T(8,128)S(1)}, f32[3,125,125]{2,1,0:T(8,128)}, u32[]{:S(2)}) copy-start(f32[3,125,125]{2,1,0:T(8,128)} %derivative_ref.1) | copy-start | bytes 562504
  2.6 1.2 %copy-start.1 = (f32[128]{0:T(128)S(1)}, f32[128]{0:T(128)}, u32[]{:S(2)}) copy-start(f32[128]{0:T(128)} %param.14) | copy-start | bytes 1540
where the time goes:
time: 79.8 us; the launch traced here: 78.6 us
  Pallas kernels  73.4 us (92%)
  local copies, waits for them, and re-layouts  4.4 us (6%)
    pallas_call x1, Pallas kernels, per_device(): pl.pallas_call(kernel, out_shape=jax.ShapeDtypeStruct(flow_state.shape, F...  73.4 us
    unnamed x13, local copies, waits for them, and re-layouts  3.07 us

commit v1 on v0

v1 whole, which is shorter than its diff:
```python
import math

import jax
import jax.numpy as jnp
from jax import lax
from jax.experimental import pallas as pl
from jax.experimental.pallas import tpu as pltpu
from jax.sharding import PartitionSpec as P

MESH = pl.DeviceIdType.MESH
F32 = jnp.float32
BF16 = jnp.bfloat16
HIGHEST = lax.Precision.HIGHEST

STAGES = 4
INST = 4
RING = 8
ROWS = 640
HALF = ROWS // 2
LANES = 128
STREAM = 32
FACE = 25


def split(value):
    high = value.astype(BF16)
    low = (value - high.astype(F32)).astype(BF16)
    return high, low


def kernel(
    flow_ref, flux_hbm, derivative_hbm, penalty_hbm, lift_hbm, frequency_ref, step_hbm, partner_hbm,
    out_ref,
    flux_ref, derivative_ref, penalty_ref, lift_ref, step_ref, partner_ref,
    x_ref, a_send, a_recv, b_send, base_ref, u_ref, ru_ref, wk_ref, wa_ref, wb_ref, wc_ref, ra_ref, rb_ref,
    sh_ref, sl_ref, r_ref, tr_send, tr_recv, t01_ref, zbuf, hbuf, dp_ref, lt_ref, pb_ref, ct_ref, g_ref, lag_ref, seen_ref, mine_ref, tau_ref,
    io_sem, small_sem, as_sem, ar_sem, bs_sem, br_sem, ts_sem, tr_sem, zs_sem, zr_sem, hs_sem, hr_sem, own_sem,
):
    inst = lax.axis_index("inst")
    row = lax.axis_index("elem")
    rows_total = lax.axis_size("elem")
    low = lax.rem(row, RING)
    high = lax.div(row, RING)
    north = lax.rem(row + 1, rows_total)
    south = lax.rem(row + rows_total - 1, rows_total)

    def inst_peer(distance):
        return lax.rem(inst + distance, INST)

    def low_peer(distance):
        return lax.rem(low + distance, RING)

    def high_peer(distance):
        return lax.rem(high + distance, RING)

    @pl.when(inst == 0)
    def _():
        for k in range(STAGES):
            tr_recv[k, 2] = jnp.zeros((2, LANES, LANES), F32)

    @pl.when(inst == INST - 1)
    def _():
        for k in range(STAGES):
            tr_recv[k, 3] = jnp.zeros((2, LANES, LANES), F32)

    barrier = pltpu.get_barrier_semaphore()
    for distance in range(1, INST):
        pl.semaphore_signal(barrier, inc=1, device_id=(inst_peer(distance), row), device_id_type=MESH)
    for other in (north, south):
        pl.semaphore_signal(barrier, inc=1, device_id=(inst, other), device_id_type=MESH)
    for distance in range(1, RING):
        pl.semaphore_signal(
            barrier, inc=1, device_id=(inst, high * RING + low_peer(distance)), device_id_type=MESH
        )
        pl.semaphore_signal(
            barrier, inc=1, device_id=(inst, high_peer(distance) * RING + low), device_id_type=MESH
        )

    loads = [
        pltpu.make_async_copy(
            flow_ref.at[:, :, half, :], x_ref.at[half, :, pl.ds(0, 125), :], io_sem.at[half]
        )
        for half in range(2)
    ]
    small = [
        pltpu.make_async_copy(source, landing, small_sem.at[place])
        for place, (source, landing) in enumerate(
            (
                (derivative_hbm, derivative_ref), (flux_hbm, flux_ref), (penalty_hbm, penalty_ref),
                (lift_hbm, lift_ref), (step_hbm, step_ref), (partner_hbm, partner_ref),
            )
        )
    ]
    for load in loads + small:
        load.start()

    lane = lax.broadcasted_iota(jnp.int32, (1, LANES), 1)

    for load in loads:
        load.wait()
    for half in range(2):
        for var in range(5):
            x_ref[half, var, 125:128, :] = jnp.zeros((3, LANES), F32)
    chunk = 40
    x_rows = x_ref.reshape(2, ROWS, LANES)

    pl.semaphore_wait(barrier, INST - 1 + 2 + 2 * (RING - 1))

    def exchange(send_buffer, recv_buffer, send_sem, recv_sem, distance):
        peer = inst_peer(distance)
        return pltpu.make_async_remote_copy(
            src_ref=send_buffer.at[peer],
            dst_ref=recv_buffer.at[inst],
            send_sem=send_sem.at[peer],
            recv_sem=recv_sem.at[inst],
            device_id=(peer, row),
            device_id_type=MESH,
        )

    def arrival(recv_buffer, send_buffer, send_sem, recv_sem, distance):
        peer = inst_peer(distance)
        return pltpu.make_async_remote_copy(
            src_ref=send_buffer.at[peer],
            dst_ref=recv_buffer.at[peer],
            send_sem=send_sem.at[peer],
            recv_sem=recv_sem.at[peer],
            device_id=(peer, row),
            device_id_type=MESH,
        )

    for distance in (2, 3, 1, 0):
        target = inst_peer(distance)
        turns = [lax.rem(STREAM * quarter + LANES - STREAM * target, LANES) for quarter in range(4)]
        for start in range(0, HALF, chunk):
            packed = None
            for quarter in range(4):
                begin = (quarter // 2) * HALF + start
                moved = pltpu.roll(x_rows[quarter % 2, begin : begin + chunk, :], turns[quarter], 1)
                packed = moved if packed is None else jnp.where(lane >= STREAM * quarter, moved, packed)
            if distance:
                a_send[target, start : start + chunk, :] = packed
            else:
                a_recv[target, start : start + chunk, :] = packed
        if distance:
            exchange(a_send, a_recv, as_sem, ar_sem, distance).start()

    for load in small:
        load.wait()

    dp_ref[...] = jnp.zeros_like(dp_ref)
    for direction in range(3):
        dp_ref[direction, 0:125, 0:125] = derivative_ref[direction]

    def volume(var, carry):
        start = pl.multiple_of(var * 128, 128)
        for other in range(5):
            block = flux_ref[var, 0:1, other : other + 1] * dp_ref[0]
            block = block + flux_ref[var, 1:2, other : other + 1] * dp_ref[1]
            block = block + flux_ref[var, 2:3, other : other + 1] * dp_ref[2]
            fine, rest = split(block)
            wk_ref[pl.ds(start, 128), other * 128 : (other + 1) * 128] = fine
            wk_ref[pl.ds(start, 128), ROWS + other * 128 : ROWS + (other + 1) * 128] = fine
            wk_ref[pl.ds(start, 128), 2 * ROWS + other * 128 : 2 * ROWS + (other + 1) * 128] = rest
        return carry

    lax.fori_loop(0, 5, volume, 0)

    face_column = lax.broadcasted_iota(jnp.int32, (FACE, LANES), 1)
    face_row = lax.broadcasted_iota(jnp.int32, (FACE, LANES), 0)
    repeat = ((lax.rem(face_column, FACE) == face_row) & (face_column < 125)).astype(F32)
    var_column = lax.broadcasted_iota(jnp.int32, (5, LANES), 1)
    var_row = lax.broadcasted_iota(jnp.int32, (5, LANES), 0)
    spread = (lax.div(var_column, FACE) == var_row).astype(F32)
    lt_ref[...] = jnp.zeros_like(lt_ref)
    for face in range(6):
        lt_ref[face, 0:125, :] = lax.dot_general(
            lift_ref[face], repeat, (((0,), (0,)), ((), ())), precision=HIGHEST, preferred_element_type=F32
        )
        pb_ref[face, 0:5, :] = jnp.dot(
            penalty_ref[:, face, :], spread, precision=HIGHEST, preferred_element_type=F32
        )
        target, place, width = (wb_ref, wa_ref, wc_ref)[face // 2], face % 2, 256
        for var in range(5):
            fine, rest = split(lt_ref[face] * pb_ref[face, var : var + 1, :])
            here = slice(var * 128, (var + 1) * 128)
            target[here, place * 128 : (place + 1) * 128] = fine
            target[here, width + place * 128 : width + (place + 1) * 128] = fine
            target[here, 2 * width + place * 128 : 2 * width + (place + 1) * 128] = rest

    g_ref[...] = jnp.zeros_like(g_ref)
    for face in range(2):
        for var in range(5):
            g_ref[face, var * 25 : var * 25 + 25, :] = (
                lt_ref[face, face * 100 : face * 100 + 25, :] * pb_ref[face, var : var + 1, :]
            )
    seen_ref[...] = jnp.zeros_like(seen_ref)
    mine_ref[...] = jnp.zeros_like(mine_ref)
    tau_ref[...] = jnp.zeros_like(tau_ref)

    to_lane = lax.broadcasted_iota(jnp.int32, (256, 256), 1)
    from_lane = lax.broadcasted_iota(jnp.int32, (256, 256), 0)
    apart = to_lane - from_lane
    turns = lax.shift_right_arithmetic(apart, 5) & 7
    aligned = (apart & 31) == 0
    spectral = jnp.zeros((256, 256), F32)
    for turn in range(1, 8):
        if turn != 4:
            weight = 0.5 * (-1) ** turn / math.tan(math.pi * turn / 8)
            spectral = jnp.where(aligned & (turns == turn), weight, spectral)
    spectral = spectral * frequency_ref[0]
    fine, rest = split(spectral)
    sh_ref[...] = fine
    sl_ref[...] = rest

    first = pltpu.roll(step_ref[...], lax.rem((INST - inst) * STREAM, LANES), 1)
    first = jnp.where(lane < STREAM, first, 0.0)
    step_lane = first + pltpu.roll(first, 32, 1) + pltpu.roll(first, 64, 1) + pltpu.roll(first, 96, 1)

    column = jnp.broadcast_to(partner_ref[0:1, :], (8, 8)).astype(F32)
    same = lax.broadcasted_iota(jnp.int32, (8, 8), 0) == lax.broadcasted_iota(jnp.int32, (8, 8), 1)
    column = jnp.sum(jnp.where(same, column, 0.0), axis=1, keepdims=True).astype(jnp.int32)
    ahead = lax.shift_right_arithmetic(jnp.broadcast_to(column, (8, LANES)), 2)
    behind = (2 * row + 128 - ahead) & 63

    t01_ref[...] = jnp.zeros_like(t01_ref)
    ct_ref[...] = jnp.zeros_like(ct_ref)
    tr_send[...] = jnp.zeros_like(tr_send)

    def unpack(side):
        for start in range(0, HALF, chunk):
            even = a_recv[2 * side, start : start + chunk, :]
            odd = a_recv[2 * side + 1, start : start + chunk, :]
            upper = jnp.where(lane < 64, even, pltpu.roll(odd, 64, 1))
            lower = jnp.where(lane < 64, pltpu.roll(even, 64, 1), odd)
            base_ref[side, start : start + chunk, :] = upper
            u_ref[side, start : start + chunk, :] = upper
            base_ref[side, HALF + start : HALF + start + chunk, :] = lower
            u_ref[side, HALF + start : HALF + start + chunk, :] = lower

    near = lax.div(inst, 2)
    for distance in (1, 3):
        @pl.when(lax.rem(inst, 2) == distance // 2)
        def _(distance=distance):
            arrival(a_recv, a_send, as_sem, ar_sem, distance).wait_recv()

    unpack(near)
    arrival(a_recv, a_send, as_sem, ar_sem, 2).wait_recv()
    for distance in (1, 3):
        @pl.when(lax.rem(inst, 2) != distance // 2)
        def _(distance=distance):
            arrival(a_recv, a_send, as_sem, ar_sem, distance).wait_recv()

    unpack(1 - near)

    stream = lane & 31

    def low_copy(k, distance, sender):
        return pltpu.make_async_remote_copy(
            src_ref=zbuf.at[k, sender],
            dst_ref=zbuf.at[k, sender],
            send_sem=zs_sem.at[k],
            recv_sem=zr_sem.at[k],
            device_id=(inst, high * RING + low_peer(distance)),
            device_id_type=MESH,
        )

    def high_copy(k, distance, sender):
        return pltpu.make_async_remote_copy(
            src_ref=hbuf.at[k, sender],
            dst_ref=hbuf.at[k, sender],
            send_sem=hs_sem.at[k],
            recv_sem=hr_sem.at[k],
            device_id=(inst, high_peer(distance) * RING + low),
            device_id_type=MESH,
        )

    def all_of(buffer, k, sem):
        every = buffer.at[k, pl.ds(0, RING - 1)]
        pltpu.make_async_copy(every, every, sem.at[k]).wait()

    def trace_copy(k, sent, landed, device):
        return pltpu.make_async_remote_copy(
            src_ref=tr_send.at[k, sent],
            dst_ref=tr_recv.at[k, landed],
            send_sem=ts_sem.at[k, sent],
            recv_sem=tr_sem.at[k, landed],
            device_id=device,
            device_id_type=MESH,
        )

    def northward(k):
        return trace_copy(k, 1, 0, (inst, north))

    def southward(k):
        return trace_copy(k, 0, 1, (inst, south))

    def upward(k):
        return trace_copy(k, 3, 2, (lax.rem(inst + 1, INST), row))

    def downward(k):
        return trace_copy(k, 2, 3, (lax.rem(inst + INST - 1, INST), row))

    has_above = inst < INST - 1
    has_below = inst > 0

    def interior_traces():
        for side in range(2):
            for var in range(5):
                t01_ref[0, side, var * 25 : var * 25 + 25, :] = u_ref[side, var * 128 : var * 128 + 25, :]
                t01_ref[1, side, var * 25 : var * 25 + 25, :] = u_ref[
                    side, var * 128 + 100 : var * 128 + 125, :
                ]

    own_tau = (step_lane[:, 15:16], step_lane[:, 16:17])

    def slide(k):
        mixed = jnp.where(
            stream == 15,
            t01_ref[1, 0],
            jnp.where(
                stream == 16,
                t01_ref[0, 0],
                jnp.where(stream == 17, pltpu.roll(t01_ref[1, 1], 2, 1), pltpu.roll(t01_ref[0, 1], 2, 1)),
            ),
        )
        ct_ref[0] = jnp.transpose(mixed)
        for kind in range(2):
            slab = jnp.concatenate(
                [ct_ref[0, pl.ds(15 + kind, 4, stride=32), :], ct_ref[0, pl.ds(17 + kind, 4, stride=32), :]], 0
            )
            zbuf[k, low, kind] = jnp.where(lane == 125, own_tau[kind], slab)
        for distance in (4, 3, 5, 2, 6, 1, 7):
            low_copy(k, distance, low).start()

    def section_weight(k):
        return jnp.where(k == 0, 0.25, jnp.where(k == 1, 1.0 / 3.0, jnp.where(k == 2, 0.5, 1.0)))

    interior_traces()
    slide(0)

    def stage(k, carry):
        weight = section_weight(k)

        for side in range(2):
            for var in range(5):
                for depth in range(5):
                    tr_send[k, 0, side, pl.ds(var * 25 + depth, 5, stride=5), :] = u_ref[
                        side, pl.ds(var * 128 + depth, 5, stride=25), :
                    ]
                    tr_send[k, 1, side, pl.ds(var * 25 + depth, 5, stride=5), :] = u_ref[
                        side, pl.ds(var * 128 + 20 + depth, 5, stride=25), :
                    ]
        northward(k).start()
        southward(k).start()
        for side in range(2):
            for var in range(5):
                tr_send[k, 2, side, var * 25 : var * 25 + 25, :] = u_ref[
                    side, pl.ds(var * 128, 25, stride=5), :
                ]
                tr_send[k, 3, side, var * 25 : var * 25 + 25, :] = u_ref[
                    side, pl.ds(var * 128 + 4, 25, stride=5), :
                ]

        @pl.when(has_above)
        def _():
            upward(k).start()

        @pl.when(has_below)
        def _():
            downward(k).start()

        @pl.when(k > 0)
        def _():
            interior_traces()

        last = section_weight(k - 1)
        returned = (
            lax.dot_general(
                jnp.concatenate([seen_ref[1], mine_ref[1]], 0), g_ref[1], (((1,), (1,)), ((), ())),
                precision=HIGHEST, preferred_element_type=F32,
            ),
            lax.dot_general(
                jnp.concatenate([seen_ref[0], mine_ref[0]], 0), g_ref[0], (((1,), (1,)), ((), ())),
                precision=HIGHEST, preferred_element_type=F32,
            ),
        )
        for kind in range(2):
            mine_ref[kind] = zbuf[k, low, kind] - (last * own_tau[kind]) * returned[kind][0:8]
            lag_ref[kind] = (last * tau_ref[kind]) * returned[kind][8:16]

        for side in range(2):
            here = slice(side * LANES, (side + 1) * LANES)
            fine, rest = split(u_ref[side])
            ru_ref[0:ROWS, here] = fine
            ru_ref[ROWS : 2 * ROWS, here] = rest
            ru_ref[2 * ROWS : 3 * ROWS, here] = fine
        r_ref[...] = jnp.dot(wk_ref[...], ru_ref[...], preferred_element_type=F32)
        r_ref[...] += jnp.dot(ru_ref[0:ROWS, :], sh_ref[...], preferred_element_type=F32)
        r_ref[...] += jnp.dot(ru_ref[ROWS : 2 * ROWS, :], sh_ref[...], preferred_element_type=F32)
        r_ref[...] += jnp.dot(ru_ref[0:ROWS, :], sl_ref[...], preferred_element_type=F32)

        for side in range(2):
            here = slice(side * LANES, (side + 1) * LANES)
            west = jnp.where((stream == 0) | (stream == 16), 0.0, pltpu.roll(t01_ref[1, side], 1, 1))
            east = jnp.where((stream == 31) | (stream == 15), 0.0, pltpu.roll(t01_ref[0, side], 127, 1))
            for face, value in ((0, west), (1, east)):
                fine, rest = split(value - t01_ref[face, side])
                rb_ref[face * 128 : (face + 1) * 128, here] = fine
                rb_ref[256 + face * 128 : 256 + (face + 1) * 128, here] = rest
                rb_ref[512 + face * 128 : 512 + (face + 1) * 128, here] = fine
        r_ref[...] += jnp.dot(wb_ref[...], rb_ref[...], preferred_element_type=F32)

        all_of(zbuf, k, zr_sem)
        rotor = zbuf[k, 0, 0]
        stator = zbuf[k, 0, 1]
        for other in range(1, RING):
            rotor = jnp.where((ahead & 7) == other, zbuf[k, other, 0], rotor)
            stator = jnp.where((behind & 7) == other, zbuf[k, other, 1], stator)
        hbuf[k, high, 0] = rotor
        hbuf[k, high, 1] = stator
        for distance in (3, 5, 2, 6, 1, 7, 4):
            high_copy(k, distance, high).start()

        @pl.when(has_below)
        def _():
            upward(k).wait_recv()

        @pl.when(has_above)
        def _():
            downward(k).wait_recv()

        def jumps(faces):
            for place, face in enumerate(faces):
                for side in range(2):
                    here = slice(side * LANES, (side + 1) * LANES)
                    fine, rest = split(tr_recv[k, face, side] - tr_send[k, face, side])
                    ra_ref[place * 128 : (place + 1) * 128, here] = fine
                    ra_ref[256 + place * 128 : 256 + (place + 1) * 128, here] = rest
                    ra_ref[512 + place * 128 : 512 + (place + 1) * 128, here] = fine

        jumps((2, 3))
        r_ref[...] += jnp.dot(wc_ref[...], ra_ref[...], preferred_element_type=F32)

        northward(k).wait_recv()
        southward(k).wait_recv()
        jumps((0, 1))
        r_ref[...] += jnp.dot(wa_ref[...], ra_ref[...], preferred_element_type=F32)

        scale = weight * step_lane
        for side in range(2):
            u_ref[side] = base_ref[side] - scale * r_ref[:, side * LANES : (side + 1) * LANES]

        @pl.when(k < STAGES - 1)
        def _():
            interior_traces()
            slide(k + 1)

        all_of(hbuf, k, hr_sem)
        rotor = hbuf[k, 0, 0]
        stator = hbuf[k, 0, 1]
        for other in range(1, RING):
            rotor = jnp.where(lax.shift_right_arithmetic(ahead, 3) == other, hbuf[k, other, 0], rotor)
            stator = jnp.where(lax.shift_right_arithmetic(behind, 3) == other, hbuf[k, other, 1], stator)

        @pl.when(k == 0)
        def _():
            tau_ref[0] = jnp.broadcast_to(rotor[:, 125:126], (8, LANES))
            tau_ref[1] = jnp.broadcast_to(stator[:, 125:126], (8, LANES))

        rotor = rotor - lag_ref[0]
        stator = stator - lag_ref[1]
        seen_ref[0] = rotor
        seen_ref[1] = stator
        ct_ref[1, pl.ds(16, 4, stride=32), :] = rotor[0:4]
        ct_ref[1, pl.ds(14, 4, stride=32), :] = rotor[4:8]
        ct_ref[1, pl.ds(15, 4, stride=32), :] = stator[0:4]
        ct_ref[1, pl.ds(13, 4, stride=32), :] = stator[4:8]
        across = jnp.transpose(ct_ref[1])
        for side in range(2):
            here = slice(side * LANES, (side + 1) * LANES)
            moved = across if side == 0 else pltpu.roll(across, 2, 1)
            for face, place in ((0, 16), (1, 15)):
                fine, rest = split(jnp.where(stream == place, moved, 0.0))
                rb_ref[face * 128 : (face + 1) * 128, here] = fine
                rb_ref[256 + face * 128 : 256 + (face + 1) * 128, here] = rest
                rb_ref[512 + face * 128 : 512 + (face + 1) * 128, here] = fine
        r_ref[...] = jnp.dot(wb_ref[...], rb_ref[...], preferred_element_type=F32)
        for side in range(2):
            u_ref[side] -= scale * r_ref[:, side * LANES : (side + 1) * LANES]

        northward(k).wait_send()
        southward(k).wait_send()

        @pl.when(has_above)
        def _():
            upward(k).wait_send()

        @pl.when(has_below)
        def _():
            downward(k).wait_send()

        all_of(zbuf, k, zs_sem)
        all_of(hbuf, k, hs_sem)
        return carry

    lax.fori_loop(0, STAGES, stage, 0)

    for distance in (2, 3, 1, 0):
        target = inst_peer(distance)
        side = lax.div(target, 2)
        turn = 64 * lax.rem(target, 2)
        for start in range(0, HALF, chunk):
            upper = pltpu.roll(u_ref[side, start : start + chunk, :], turn, 1)
            lower = pltpu.roll(u_ref[side, HALF + start : HALF + start + chunk, :], 64 - turn, 1)
            packed = jnp.where(lane < 64, upper, lower)
            b_send[target, start : start + chunk, :] = packed
        if distance:
            exchange(b_send, out_ref, bs_sem, br_sem, distance).start()
    own = pltpu.make_async_copy(b_send.at[inst], out_ref.at[inst], own_sem)
    own.start()
    for distance in range(1, INST):
        exchange(a_send, a_recv, as_sem, ar_sem, distance).wait_send()
    for distance in range(1, INST):
        exchange(b_send, out_ref, bs_sem, br_sem, distance).wait_send()
    own.wait()
    for distance in (1, 3, 2):
        arrival(out_ref, b_send, bs_sem, br_sem, distance).wait_recv()


def finish(parts_hbm, out_ref, parts_ref, x_ref, in_sem, out_sem):
    lane = lax.broadcasted_iota(jnp.int32, (1, LANES), 1)
    pieces = 4
    piece = HALF // pieces
    loads = [
        pltpu.make_async_copy(
            parts_hbm.at[:, pl.ds(part * piece, piece), :], parts_ref.at[:, pl.ds(part * piece, piece), :],
            in_sem.at[part],
        )
        for part in range(pieces)
    ]

    def store(var):
        return [
            pltpu.make_async_copy(
                x_ref.at[half, pl.ds(var * 128, 125), :], out_ref.at[var, :, half, :], out_sem.at[half * 5 + var]
            )
            for half in range(2)
        ]

    for load in loads:
        load.start()
    for part in range(pieces):
        loads[part].wait()
        for start in range(part * piece, (part + 1) * piece, 40):
            parts = [parts_ref[source, start : start + 40, :] for source in range(INST)]
            for quarter in range(4):
                whole = None
                for source in range(INST):
                    turn = (STREAM * (source - quarter)) % LANES
                    moved = parts[source] if turn == 0 else pltpu.roll(parts[source], turn, 1)
                    whole = moved if whole is None else jnp.where(lane >= STREAM * source, moved, whole)
                begin = (quarter // 2) * HALF + start
                x_ref[quarter % 2, begin : begin + 40, :] = whole
        for var in ((), (0,), (3,), (1, 2, 4))[part]:
            for copy in store(var):
                copy.start()
    for var in range(5):
        for copy in store(var):
            copy.wait()


def per_device(
    flow_state, flux_matrices, derivative, penalty, lift_matrices, frequency, step_size, partner
):
    outside = pl.BlockSpec(memory_space=pltpu.HBM)
    scalar = pl.BlockSpec(memory_space=pltpu.SMEM)
    dma = pltpu.SemaphoreType.DMA
    parts = pl.pallas_call(
        kernel,
        out_shape=jax.ShapeDtypeStruct((INST, HALF, LANES), F32),
        in_specs=[outside, outside, outside, outside, outside, scalar, outside, outside],
        out_specs=outside,
        scratch_shapes=[
            pltpu.VMEM((5, 3, 5), F32),
            pltpu.VMEM((3, 125, 125), F32),
            pltpu.VMEM((5, 6, 5), F32),
            pltpu.VMEM((6, FACE, 125), F32),
            pltpu.VMEM((1, LANES), F32),
            pltpu.VMEM((4, 8), jnp.int32),
            pltpu.VMEM((2, 5, LANES, LANES), F32),
            pltpu.VMEM((INST, HALF, LANES), F32),
            pltpu.VMEM((INST, HALF, LANES), F32),
            pltpu.VMEM((INST, HALF, LANES), F32),
            pltpu.VMEM((2, ROWS, LANES), F32),
            pltpu.VMEM((2, ROWS, LANES), F32),
            pltpu.VMEM((3 * ROWS, 256), BF16),
            pltpu.VMEM((ROWS, 3 * ROWS), BF16),
            pltpu.VMEM((ROWS, 3 * 256), BF16),
            pltpu.VMEM((ROWS, 3 * 256), BF16),
            pltpu.VMEM((ROWS, 3 * 256), BF16),
            pltpu.VMEM((3 * 256, 256), BF16),
            pltpu.VMEM((3 * 256, 256), BF16),
            pltpu.VMEM((256, 256), BF16),
            pltpu.VMEM((256, 256), BF16),
            pltpu.VMEM((ROWS, 256), F32),
            pltpu.VMEM((STAGES, 4, 2, LANES, LANES), F32),
            pltpu.VMEM((STAGES, 4, 2, LANES, LANES), F32),
            pltpu.VMEM((2, 2, LANES, LANES), F32),
            pltpu.VMEM((STAGES, RING, 2, 8, LANES), F32),
            pltpu.VMEM((STAGES, RING, 2, 8, LANES), F32),
            pltpu.VMEM((3, LANES, LANES), F32),
            pltpu.VMEM((6, LANES, LANES), F32),
            pltpu.VMEM((6, 8, LANES), F32),
            pltpu.VMEM((2, LANES, LANES), F32),
            pltpu.VMEM((2, LANES, LANES), F32),
            pltpu.VMEM((2, 8, LANES), F32),
            pltpu.VMEM((2, 8, LANES), F32),
            pltpu.VMEM((2, 8, LANES), F32),
            pltpu.VMEM((2, 8, LANES), F32),
            dma((2,)),
            dma((6,)),
            dma((INST,)),
            dma((INST,)),
            dma((INST,)),
            dma((INST,)),
            dma((STAGES, 4)),
            dma((STAGES, 4)),
            dma((STAGES,)),
            dma((STAGES,)),
            dma((STAGES,)),
            dma((STAGES,)),
            dma,
        ],
        compiler_params=pltpu.CompilerParams(
            collective_id=0, has_side_effects=True, vmem_limit_bytes=67_043_328
        ),
    )(
        jnp.transpose(flow_state, (1, 2, 0, 3)), jnp.transpose(flux_matrices, (1, 0, 2)), derivative,
        jnp.transpose(penalty, (1, 0, 2)), jnp.transpose(lift_matrices, (0, 2, 1)), frequency,
        step_size.reshape(1, LANES), jnp.transpose(partner, (1, 0)),
    )
    result = pl.pallas_call(
        finish,
        out_shape=jax.ShapeDtypeStruct((5, 125, 2, LANES), F32),
        in_specs=[outside],
        out_specs=outside,
        scratch_shapes=[
            pltpu.VMEM((INST, HALF, LANES), F32),
            pltpu.VMEM((2, ROWS, LANES), F32),
            dma((4,)),
            dma((10,)),
        ],
        compiler_params=pltpu.CompilerParams(vmem_limit_bytes=67_043_328),
    )(parts)
    return jnp.transpose(result, (2, 0, 1, 3))


def solution(mesh):
    placed = (P("inst", None, None, "elem"), P(), P(), P(), P(), P(), P("elem"), P(None, "elem"))
    return jax.shard_map(
        per_device,
        mesh=mesh,
        in_specs=placed,
        out_specs=P("inst", None, None, "elem"),
        check_vma=False,
    )
```

time: 79.8 us -> 68.9 us (0.86)
  Pallas kernels: 73.4 us -> 67.6 us
  local copies, waits for them, and re-layouts: 4.4 us -> 0 us
    pallas_call x1 -> x2, Pallas kernels: 73.4 us -> 67.6 us  [the longest x1 65.1 us: per_device(): pl.pallas_call(kernel, out_shape=jax.ShapeDtypeStruct((INST, HALF, LANES)...]
    unnamed x13 -> x0, local copies, waits for them, and re-layouts: 3.07 us -> none
    pallas_call x1 -> x0, local copies, waits for them, and re-layouts: 1.33 us -> none  [per_device(): pl.pallas_call(kernel, out_shape=jax.ShapeDtypeStruct(flow_state.shape, F...]
where the time goes in v1:
time: 68.9 us; the launch traced here: 68.3 us
  Pallas kernels  67.6 us (98%)
    pallas_call x1, Pallas kernels, per_device(): pl.pallas_call(kernel, out_shape=jax.ShapeDtypeStruct((INST, HALF, LANES)...  65.1 us
    pallas_call x1, Pallas kernels, per_device(): pl.pallas_call(finish, out_shape=jax.ShapeDtypeStruct((5, 125, 2, LANES),...  2.55 us

profile of v1, /device:TPU:1, one launch (start us, length us, event | category | flops | bytes accessed | tf_op | source)
XLA Modules:
  0.0 68.3 jit_solution(10649161023933059253)
XLA Ops:
  0.7 65.1 %shard_map.82.parts_hbm = f32[4,320,128]{2,1,0:T(8,128)} custom-call(f32[5,125,2,128]{3,2,1,0:T(2,128)} %bitcast.7, f32[5,3,5]{2,1,0:T(4,128)} %bitcast.10, f32[3,125,125]{2,1,0:T(8,128)} %derivative_hbm.1, f32[5,6,5]{2,1,0:T(8,128)} %bitcast.9, f32[6,25,125]{2,1,0:T(8,128)} %bitcast.8, f32[1]{0:T(128)S(6)} %copy.9.frequency_ref, f32[1,128]{1,0:T(1,128)} %bitcast.12, ...), custom_call_target="tpu_custom_call" | custom-call | tf_op jit(solution)/shard_map/pallas_call | solution.py:578
  65.7 2.5 %shard_map.83 = f32[5,125,2,128]{3,2,1,0:T(2,128)} custom-call(f32[4,320,128]{2,1,0:T(8,128)} %shard_map.82.parts_hbm), custom_call_target="tpu_custom_call" | custom-call | tf_op jit(solution)/shard_map/pallas_call | solution.py:642

commit v2 on v1

v2 whole, which is shorter than its diff:
```python
import math

import jax
import jax.numpy as jnp
from jax import lax
from jax.experimental import pallas as pl
from jax.experimental.pallas import tpu as pltpu
from jax.sharding import PartitionSpec as P

MESH = pl.DeviceIdType.MESH
F32 = jnp.float32
BF16 = jnp.bfloat16
HIGHEST = lax.Precision.HIGHEST

STAGES = 4
INST = 4
RING = 8
ROWS = 640
HALF = ROWS // 2
LANES = 128
STREAM = 32
FACE = 25


def split(value):
    high = value.astype(BF16)
    low = (value - high.astype(F32)).astype(BF16)
    return high, low


def halves(left, right):
    middle = left.shape[0] // 2
    return jnp.concatenate(
        [
            jnp.dot(left[:middle, :], right[...], preferred_element_type=F32),
            jnp.dot(left[middle:, :], right[...], preferred_element_type=F32),
        ],
        0,
    )


def kernel(
    flow_ref, flux_hbm, derivative_hbm, penalty_hbm, lift_hbm, frequency_hbm, step_hbm, partner_hbm,
    out_ref,
    flux_ref, derivative_ref, penalty_ref, lift_ref, step_ref, partner_ref, frequency_ref,
    x_ref, a_send, a_recv, b_send, base_ref, u_ref, ru_ref, wk_ref, wa_ref, wb_ref, wc_ref, ra_ref, rb_ref,
    sh_ref, sl_ref, r_ref, tr_send, tr_recv, t01_ref, zbuf, hbuf, dp_ref, lt_ref, pb_ref, ct_ref, g_ref, lag_ref, seen_ref, mine_ref, tau_ref,
    io_sem, small_sem, as_sem, ar_sem, bs_sem, br_sem, ps_sem, us_sem, ds_sem, zs_sem, hs_sem,
    pr_sem, ur_sem, dr_sem, zr_sem, hr_sem, own_sem,
):
    inst = lax.axis_index("inst")
    row = lax.axis_index("elem")
    rows_total = lax.axis_size("elem")
    low = lax.rem(row, RING)
    high = lax.div(row, RING)
    north = lax.rem(row + 1, rows_total)
    south = lax.rem(row + rows_total - 1, rows_total)

    def inst_peer(distance):
        return lax.rem(inst + distance, INST)

    def low_peer(distance):
        return lax.rem(low + distance, RING)

    def high_peer(distance):
        return lax.rem(high + distance, RING)

    @pl.when(inst == 0)
    def _():
        for k in range(STAGES):
            tr_recv[k, :, 2] = jnp.zeros((2, LANES, LANES), F32)

    @pl.when(inst == INST - 1)
    def _():
        for k in range(STAGES):
            tr_recv[k, :, 3] = jnp.zeros((2, LANES, LANES), F32)

    barrier = pltpu.get_barrier_semaphore()
    for distance in range(1, INST):
        pl.semaphore_signal(barrier, inc=1, device_id=(inst_peer(distance), row), device_id_type=MESH)
    for other in (north, south):
        pl.semaphore_signal(barrier, inc=1, device_id=(inst, other), device_id_type=MESH)
    for distance in range(1, RING):
        pl.semaphore_signal(
            barrier, inc=1, device_id=(inst, high * RING + low_peer(distance)), device_id_type=MESH
        )
        pl.semaphore_signal(
            barrier, inc=1, device_id=(inst, high_peer(distance) * RING + low), device_id_type=MESH
        )

    loads = [
        pltpu.make_async_copy(
            flow_ref.at[:, :, half, :], x_ref.at[half, :, pl.ds(0, 125), :], io_sem.at[half]
        )
        for half in range(2)
    ]
    small = [
        pltpu.make_async_copy(source, landing, small_sem.at[place])
        for place, (source, landing) in enumerate(
            (
                (derivative_hbm, derivative_ref), (flux_hbm, flux_ref), (penalty_hbm, penalty_ref),
                (lift_hbm, lift_ref), (step_hbm, step_ref), (partner_hbm, partner_ref),
                (frequency_hbm, frequency_ref),
            )
        )
    ]
    for load in loads + small:
        load.start()

    lane = lax.broadcasted_iota(jnp.int32, (1, LANES), 1)

    for load in loads:
        load.wait()
    for half in range(2):
        for var in range(5):
            x_ref[half, var, 125:128, :] = jnp.zeros((3, LANES), F32)
    chunk = 40
    x_rows = x_ref.reshape(2, ROWS, LANES)

    pl.semaphore_wait(barrier, INST - 1 + 2 + 2 * (RING - 1))

    partner_inst = inst + 1 - 2 * lax.rem(inst, 2)
    peers = (inst_peer(2), INST - 1 - inst, partner_inst, inst)

    def exchange(send_buffer, recv_buffer, send_sem, recv_sem, peer):
        return pltpu.make_async_remote_copy(
            src_ref=send_buffer.at[peer],
            dst_ref=recv_buffer.at[inst],
            send_sem=send_sem,
            recv_sem=recv_sem.at[inst],
            device_id=(peer, row),
            device_id_type=MESH,
        )

    def arrival(recv_buffer, send_buffer, send_sem, recv_sem, peer):
        return pltpu.make_async_remote_copy(
            src_ref=send_buffer.at[peer],
            dst_ref=recv_buffer.at[peer],
            send_sem=send_sem,
            recv_sem=recv_sem.at[peer],
            device_id=(peer, row),
            device_id_type=MESH,
        )

    for order, target in enumerate(peers):
        remote = order < INST - 1
        turns = [lax.rem(STREAM * quarter + LANES - STREAM * target, LANES) for quarter in range(4)]
        for start in range(0, HALF, chunk):
            packed = None
            for quarter in range(4):
                begin = (quarter // 2) * HALF + start
                moved = pltpu.roll(x_rows[quarter % 2, begin : begin + chunk, :], turns[quarter], 1)
                packed = moved if packed is None else jnp.where(lane >= STREAM * quarter, moved, packed)
            if remote:
                a_send[target, start : start + chunk, :] = packed
            else:
                a_recv[target, start : start + chunk, :] = packed
        if remote:
            exchange(a_send, a_recv, as_sem, ar_sem, target).start()

    for load in small:
        load.wait()

    dp_ref[...] = jnp.zeros_like(dp_ref)
    for direction in range(3):
        dp_ref[direction, 0:125, 0:125] = derivative_ref[direction]

    def volume(var, carry):
        start = pl.multiple_of(var * 128, 128)
        for other in range(5):
            block = flux_ref[var, 0:1, other : other + 1] * dp_ref[0]
            block = block + flux_ref[var, 1:2, other : other + 1] * dp_ref[1]
            block = block + flux_ref[var, 2:3, other : other + 1] * dp_ref[2]
            fine, rest = split(block)
            wk_ref[pl.ds(start, 128), other * 128 : (other + 1) * 128] = fine
            wk_ref[pl.ds(start, 128), ROWS + other * 128 : ROWS + (other + 1) * 128] = fine
            wk_ref[pl.ds(start, 128), 2 * ROWS + other * 128 : 2 * ROWS + (other + 1) * 128] = rest
        return carry

    lax.fori_loop(0, 5, volume, 0)

    face_column = lax.broadcasted_iota(jnp.int32, (FACE, LANES), 1)
    face_row = lax.broadcasted_iota(jnp.int32, (FACE, LANES), 0)
    repeat = ((lax.rem(face_column, FACE) == face_row) & (face_column < 125)).astype(F32)
    var_column = lax.broadcasted_iota(jnp.int32, (5, LANES), 1)
    var_row = lax.broadcasted_iota(jnp.int32, (5, LANES), 0)
    spread = (lax.div(var_column, FACE) == var_row).astype(F32)
    lt_ref[...] = jnp.zeros_like(lt_ref)
    for face in range(6):
        lt_ref[face, 0:125, :] = lax.dot_general(
            lift_ref[face], repeat, (((0,), (0,)), ((), ())), precision=HIGHEST, preferred_element_type=F32
        )
        pb_ref[face, 0:5, :] = jnp.dot(
            penalty_ref[:, face, :], spread, precision=HIGHEST, preferred_element_type=F32
        )
        target, place, width = (wb_ref, wa_ref, wc_ref)[face // 2], face % 2, 256
        for var in range(5):
            fine, rest = split(lt_ref[face] * pb_ref[face, var : var + 1, :])
            here = slice(var * 128, (var + 1) * 128)
            target[here, place * 128 : (place + 1) * 128] = fine
            target[here, width + place * 128 : width + (place + 1) * 128] = fine
            target[here, 2 * width + place * 128 : 2 * width + (place + 1) * 128] = rest

    g_ref[...] = jnp.zeros_like(g_ref)
    for face in range(2):
        for var in range(5):
            g_ref[face, var * 25 : var * 25 + 25, :] = (
                lt_ref[face, face * 100 : face * 100 + 25, :] * pb_ref[face, var : var + 1, :]
            )
    seen_ref[...] = jnp.zeros_like(seen_ref)
    mine_ref[...] = jnp.zeros_like(mine_ref)
    tau_ref[...] = jnp.zeros_like(tau_ref)

    to_lane = lax.broadcasted_iota(jnp.int32, (256, 256), 1)
    from_lane = lax.broadcasted_iota(jnp.int32, (256, 256), 0)
    apart = to_lane - from_lane
    turns = lax.shift_right_arithmetic(apart, 5) & 7
    aligned = (apart & 31) == 0
    spectral = jnp.zeros((256, 256), F32)
    for turn in range(1, 8):
        if turn != 4:
            weight = 0.5 * (-1) ** turn / math.tan(math.pi * turn / 8)
            spectral = jnp.where(aligned & (turns == turn), weight, spectral)
    spectral = spectral * frequency_ref[...]
    fine, rest = split(spectral)
    sh_ref[...] = fine
    sl_ref[...] = rest

    first = pltpu.roll(step_ref[...], lax.rem((INST - inst) * STREAM, LANES), 1)
    first = jnp.where(lane < STREAM, first, 0.0)
    step_lane = first + pltpu.roll(first, 32, 1) + pltpu.roll(first, 64, 1) + pltpu.roll(first, 96, 1)

    column = jnp.broadcast_to(partner_ref[0:1, :], (8, 8)).astype(F32)
    same = lax.broadcasted_iota(jnp.int32, (8, 8), 0) == lax.broadcasted_iota(jnp.int32, (8, 8), 1)
    column = jnp.sum(jnp.where(same, column, 0.0), axis=1, keepdims=True).astype(jnp.int32)
    ahead = lax.shift_right_arithmetic(jnp.broadcast_to(column, (8, LANES)), 2)
    behind = (2 * row + 128 - ahead) & 63

    wanted = tuple(
        jnp.concatenate([ahead[4 * side : 4 * side + 4], behind[4 * side : 4 * side + 4]], 0) for side in range(2)
    )

    t01_ref[...] = jnp.zeros_like(t01_ref)
    ct_ref[...] = jnp.zeros_like(ct_ref)
    tr_send[...] = jnp.zeros_like(tr_send)

    def unpack(side):
        for start in range(0, HALF, chunk):
            even = a_recv[2 * side, start : start + chunk, :]
            odd = a_recv[2 * side + 1, start : start + chunk, :]
            upper = jnp.where(lane < 64, even, pltpu.roll(odd, 64, 1))
            lower = jnp.where(lane < 64, pltpu.roll(even, 64, 1), odd)
            base_ref[side, start : start + chunk, :] = upper
            u_ref[side, start : start + chunk, :] = upper
            base_ref[side, HALF + start : HALF + start + chunk, :] = lower
            u_ref[side, HALF + start : HALF + start + chunk, :] = lower

    stream = lane & 31
    eighth = lax.broadcasted_iota(jnp.int32, (8, LANES), 0)
    own_tau = jnp.where(eighth < 4, step_lane[:, 15:16], step_lane[:, 16:17])
    near = lax.div(inst, 2)
    far = 1 - near

    def hop(buffer, k, side, sender, send_sem, recv_sem, device):
        return pltpu.make_async_remote_copy(
            src_ref=buffer.at[k, side, sender],
            dst_ref=buffer.at[k, side, sender],
            send_sem=send_sem,
            recv_sem=recv_sem.at[k, side],
            device_id=(inst, device),
            device_id_type=MESH,
        )

    def all_of(part, sem):
        pltpu.make_async_copy(part, part, sem).wait()

    def trace_copy(k, side, sent, landed, send_sem, recv_sem, device):
        return pltpu.make_async_remote_copy(
            src_ref=tr_send.at[k, side, sent],
            dst_ref=tr_recv.at[k, side, landed],
            send_sem=send_sem,
            recv_sem=recv_sem.at[k, side],
            device_id=device,
            device_id_type=MESH,
        )

    def upward(k, side):
        return trace_copy(k, side, 3, 2, us_sem, ur_sem, (lax.rem(inst + 1, INST), row))

    def downward(k, side):
        return trace_copy(k, side, 2, 3, ds_sem, dr_sem, (lax.rem(inst + INST - 1, INST), row))

    has_above = inst < INST - 1
    has_below = inst > 0

    def interior_traces(side):
        for var in range(5):
            t01_ref[0, side, var * 25 : var * 25 + 25, :] = u_ref[side, var * 128 : var * 128 + 25, :]
            t01_ref[1, side, var * 25 : var * 25 + 25, :] = u_ref[side, var * 128 + 100 : var * 128 + 125, :]

    def slide(k, side):
        ct_ref[0] = jnp.transpose(jnp.where(stream == 15, t01_ref[1, side], t01_ref[0, side]))
        slab = jnp.concatenate([ct_ref[0, pl.ds(15 + kind, 4, stride=32), :] for kind in range(2)], 0)
        zbuf[k, side, low] = jnp.where(lane == 125, own_tau, slab)
        for distance in (4, 3, 5, 2, 6, 1, 7):
            hop(zbuf, k, side, low, zs_sem, zr_sem, high * RING + low_peer(distance)).start()

    def send_traces(k, side):
        for var in range(5):
            for depth in range(5):
                for face in range(2):
                    tr_send[k, side, face, pl.ds(var * 25 + depth, 5, stride=5), :] = u_ref[
                        side, pl.ds(var * 128 + 20 * face + depth, 5, stride=25), :
                    ]
        trace_copy(k, side, 1, 0, ps_sem, pr_sem, (inst, north)).start()
        trace_copy(k, side, 0, 1, ps_sem, pr_sem, (inst, south)).start()
        for var in range(5):
            for face in range(2):
                tr_send[k, side, 2 + face, var * 25 : var * 25 + 25, :] = u_ref[
                    side, pl.ds(var * 128 + 4 * face, 25, stride=5), :
                ]

        @pl.when(has_above)
        def _():
            upward(k, side).start()

        @pl.when(has_below)
        def _():
            downward(k, side).start()

    def begin(side):
        unpack(side)
        interior_traces(side)
        slide(0, side)
        send_traces(0, side)

    arrival(a_recv, a_send, as_sem, ar_sem, partner_inst).wait_recv()
    begin(near)
    for peer in peers[:2]:
        arrival(a_recv, a_send, as_sem, ar_sem, peer).wait_recv()
    begin(far)

    def section_weight(k):
        return jnp.where(k == 0, 0.25, jnp.where(k == 1, 1.0 / 3.0, jnp.where(k == 2, 0.5, 1.0)))

    def pick(buffer, k, side, digit):
        wanted_here = jnp.where(side == 0, wanted[0], wanted[1])
        digits = wanted_here & 7 if digit == 0 else lax.shift_right_arithmetic(wanted_here, 3)
        picked = buffer[k, side, 0]
        for other in range(1, RING):
            picked = jnp.where(digits == other, buffer[k, side, other], picked)
        return picked

    def place(target, start, value):
        fine, rest = split(value)
        target[start : start + 128, :] = fine
        target[256 + start : 256 + start + 128, :] = rest
        target[512 + start : 512 + start + 128, :] = fine

    def stage(k, carry):
        weight = section_weight(k)
        last = section_weight(k - 1)
        scale = weight * step_lane

        @pl.when(k > 0)
        def _():
            interior_traces(0)
            interior_traces(1)

        known = jnp.concatenate([seen_ref[0], mine_ref[0], seen_ref[1], mine_ref[1]], 0)
        through = [
            lax.dot_general(
                known, g_ref[face], (((1,), (1,)), ((), ())), precision=HIGHEST, preferred_element_type=F32
            )
            for face in range(2)
        ]
        for side in range(2):
            back = [
                jnp.concatenate([through[1][start + 4 : start + 8], through[0][start : start + 4]], 0)
                for start in (16 * side, 16 * side + 8)
            ]
            mine_ref[side] = zbuf[k, side, low] - (last * own_tau) * back[0]
            lag_ref[side] = (last * tau_ref[side]) * back[1]

        for side in range(2):
            here = slice(side * LANES, (side + 1) * LANES)
            fine, rest = split(u_ref[side])
            ru_ref[0:ROWS, here] = fine
            ru_ref[ROWS : 2 * ROWS, here] = rest
            ru_ref[2 * ROWS : 3 * ROWS, here] = fine
            west = jnp.where((stream == 0) | (stream == 16), 0.0, pltpu.roll(t01_ref[1, side], 1, 1))
            east = jnp.where((stream == 31) | (stream == 15), 0.0, pltpu.roll(t01_ref[0, side], 127, 1))
            for face, value in ((0, west), (1, east)):
                fine, rest = split(value - t01_ref[face, side])
                rb_ref[face * 128 : (face + 1) * 128, here] = fine
                rb_ref[256 + face * 128 : 256 + (face + 1) * 128, here] = rest
                rb_ref[512 + face * 128 : 512 + (face + 1) * 128, here] = fine

        def add(left, right, first=False):
            both = halves(left, right)
            for side in range(2):
                part = both[:, side * LANES : (side + 1) * LANES]
                if first:
                    r_ref[side] = part
                else:
                    r_ref[side] += part

        add(wk_ref, ru_ref, True)
        add(ru_ref.at[0:ROWS], sh_ref)
        add(ru_ref.at[ROWS : 2 * ROWS], sh_ref)
        add(ru_ref.at[0:ROWS], sl_ref)
        add(wb_ref, rb_ref)

        for side in (near, far):
            all_of(zbuf.at[k, side, pl.ds(0, RING - 1)], zr_sem.at[k, side])
            hbuf[k, side, high] = pick(zbuf, k, side, 0)
            for distance in (3, 5, 2, 6, 1, 7, 4):
                hop(hbuf, k, side, high, hs_sem, hr_sem, high_peer(distance) * RING + low).start()

        for side in (near, far):
            @pl.when(has_below)
            def _(side=side):
                upward(k, side).wait_recv()

            @pl.when(has_above)
            def _(side=side):
                downward(k, side).wait_recv()

            for face in range(2):
                place(ra_ref, face * 128, tr_recv[k, side, 2 + face] - tr_send[k, side, 2 + face])
            r_ref[side] += halves(wc_ref, ra_ref)
            all_of(tr_recv.at[k, side, pl.ds(0, 2)], pr_sem.at[k, side])
            for face in range(2):
                place(ra_ref, face * 128, tr_recv[k, side, face] - tr_send[k, side, face])
            total = r_ref[side] + halves(wa_ref, ra_ref)
            u_ref[side] = base_ref[side] - scale * total

            @pl.when(k < STAGES - 1)
            def _(side=side):
                interior_traces(side)
                slide(k + 1, side)

        for side in (near, far):
            all_of(hbuf.at[k, side, pl.ds(0, RING - 1)], hr_sem.at[k, side])
            seen = pick(hbuf, k, side, 1)

            @pl.when(k == 0)
            def _(side=side, seen=seen):
                tau_ref[side] = jnp.broadcast_to(seen[:, 125:126], (8, LANES))

            seen = seen - lag_ref[side]
            seen_ref[side] = seen
            ct_ref[1, pl.ds(16, 4, stride=32), :] = seen[0:4]
            ct_ref[1, pl.ds(15, 4, stride=32), :] = seen[4:8]
            across = jnp.transpose(ct_ref[1])
            for face in range(2):
                place(ra_ref, face * 128, jnp.where(stream == 16 - face, across, 0.0))
            u_ref[side] -= scale * halves(wb_ref, ra_ref)

            @pl.when(k < STAGES - 1)
            def _(side=side):
                send_traces(k + 1, side)
        return carry

    lax.fori_loop(0, STAGES, stage, 0)

    for order, target in enumerate(peers):
        side = lax.div(target, 2)
        turn = 64 * lax.rem(target, 2)
        for start in range(0, HALF, chunk):
            upper = pltpu.roll(u_ref[side, start : start + chunk, :], turn, 1)
            lower = pltpu.roll(u_ref[side, HALF + start : HALF + start + chunk, :], 64 - turn, 1)
            packed = jnp.where(lane < 64, upper, lower)
            b_send[target, start : start + chunk, :] = packed
        if order < INST - 1:
            exchange(b_send, out_ref, bs_sem, br_sem, target).start()
    own = pltpu.make_async_copy(b_send.at[inst], out_ref.at[inst], own_sem)
    own.start()
    all_of(a_send.at[pl.ds(0, INST - 1)], as_sem)
    all_of(b_send.at[pl.ds(0, INST - 1)], bs_sem)
    all_of(zbuf.at[:, :, pl.ds(0, RING - 1)], zs_sem)
    all_of(hbuf.at[:, :, pl.ds(0, RING - 1)], hs_sem)
    all_of(tr_send.at[:, :, pl.ds(0, 2)], ps_sem)

    @pl.when(has_above)
    def _():
        all_of(tr_send.at[:, :, 3], us_sem)

    @pl.when(has_below)
    def _():
        all_of(tr_send.at[:, :, 2], ds_sem)

    own.wait()
    for peer in peers[:3]:
        arrival(out_ref, b_send, bs_sem, br_sem, peer).wait_recv()


def finish(parts_hbm, out_ref, parts_ref, x_ref, in_sem, out_sem):
    lane = lax.broadcasted_iota(jnp.int32, (1, LANES), 1)
    pieces = 4
    piece = HALF // pieces
    loads = [
        pltpu.make_async_copy(
            parts_hbm.at[:, pl.ds(part * piece, piece), :], parts_ref.at[:, pl.ds(part * piece, piece), :],
            in_sem.at[part],
        )
        for part in range(pieces)
    ]

    def runs(part):
        found = []
        for upper in range(2):
            first, end = upper * HALF + part * piece, upper * HALF + (part + 1) * piece
            while first < end:
                var, node = divmod(first, 128)
                stop = min(end, (var + 1) * 128)
                found.append((var, node, min(stop, var * 128 + 125) - first))
                first = stop
        return found

    for load in loads:
        load.start()
    for part in range(pieces):
        loads[part].wait()
        for start in range(part * piece, (part + 1) * piece, 40):
            parts = [parts_ref[source, start : start + 40, :] for source in range(INST)]
            for quarter in range(4):
                whole = None
                for source in range(INST):
                    turn = (STREAM * (source - quarter)) % LANES
                    moved = parts[source] if turn == 0 else pltpu.roll(parts[source], turn, 1)
                    whole = moved if whole is None else jnp.where(lane >= STREAM * source, moved, whole)
                begin = (quarter // 2) * HALF + start
                x_ref[quarter % 2, begin : begin + 40, :] = whole
        for var, node, count in runs(part):
            for half in range(2):
                pltpu.make_async_copy(
                    x_ref.at[half, pl.ds(var * 128 + node, count), :],
                    out_ref.at[var, pl.ds(node, count), half, :],
                    out_sem.at[part],
                ).start()
    for part in range(pieces):
        every = x_ref.at[0, pl.ds(0, 2 * sum(count for _, _, count in runs(part))), :]
        pltpu.make_async_copy(every, every, out_sem.at[part]).wait()


def per_device(
    flow_state, flux_matrices, derivative, penalty, lift_matrices, frequency, step_size, partner
):
    outside = pl.BlockSpec(memory_space=pltpu.HBM)
    dma = pltpu.SemaphoreType.DMA
    parts = pl.pallas_call(
        kernel,
        out_shape=jax.ShapeDtypeStruct((INST, HALF, LANES), F32),
        in_specs=[outside, outside, outside, outside, outside, outside, outside, outside],
        out_specs=outside,
        scratch_shapes=[
            pltpu.VMEM((5, 3, 5), F32),
            pltpu.VMEM((3, 125, 125), F32),
            pltpu.VMEM((5, 6, 5), F32),
            pltpu.VMEM((6, FACE, 125), F32),
            pltpu.VMEM((1, LANES), F32),
            pltpu.VMEM((4, 8), jnp.int32),
            pltpu.VMEM((1, 1), F32),
            pltpu.VMEM((2, 5, LANES, LANES), F32),
            pltpu.VMEM((INST, HALF, LANES), F32),
            pltpu.VMEM((INST, HALF, LANES), F32),
            pltpu.VMEM((INST, HALF, LANES), F32),
            pltpu.VMEM((2, ROWS, LANES), F32),
            pltpu.VMEM((2, ROWS, LANES), F32),
            pltpu.VMEM((3 * ROWS, 256), BF16),
            pltpu.VMEM((ROWS, 3 * ROWS), BF16),
            pltpu.VMEM((ROWS, 3 * 256), BF16),
            pltpu.VMEM((ROWS, 3 * 256), BF16),
            pltpu.VMEM((ROWS, 3 * 256), BF16),
            pltpu.VMEM((3 * 256, LANES), BF16),
            pltpu.VMEM((3 * 256, 256), BF16),
            pltpu.VMEM((256, 256), BF16),
            pltpu.VMEM((256, 256), BF16),
            pltpu.VMEM((2, ROWS, LANES), F32),
            pltpu.VMEM((STAGES, 2, 4, LANES, LANES), F32),
            pltpu.VMEM((STAGES, 2, 4, LANES, LANES), F32),
            pltpu.VMEM((2, 2, LANES, LANES), F32),
            pltpu.VMEM((STAGES, 2, RING, 8, LANES), F32),
            pltpu.VMEM((STAGES, 2, RING, 8, LANES), F32),
            pltpu.VMEM((3, LANES, LANES), F32),
            pltpu.VMEM((6, LANES, LANES), F32),
            pltpu.VMEM((6, 8, LANES), F32),
            pltpu.VMEM((2, LANES, LANES), F32),
            pltpu.VMEM((2, LANES, LANES), F32),
            pltpu.VMEM((2, 8, LANES), F32),
            pltpu.VMEM((2, 8, LANES), F32),
            pltpu.VMEM((2, 8, LANES), F32),
            pltpu.VMEM((2, 8, LANES), F32),
            dma((2,)),
            dma((7,)),
            dma,
            dma((INST,)),
            dma,
            dma((INST,)),
            dma,
            dma,
            dma,
            dma,
            dma,
            dma((STAGES, 2)),
            dma((STAGES, 2)),
            dma((STAGES, 2)),
            dma((STAGES, 2)),
            dma((STAGES, 2)),
            dma,
        ],
        compiler_params=pltpu.CompilerParams(
            collective_id=0, has_side_effects=True, vmem_limit_bytes=67_043_328
        ),
    )(
        jnp.transpose(flow_state, (1, 2, 0, 3)), jnp.transpose(flux_matrices, (1, 0, 2)), derivative,
        jnp.transpose(penalty, (1, 0, 2)), jnp.transpose(lift_matrices, (0, 2, 1)),
        frequency.reshape(1, 1),
        step_size.reshape(1, LANES), jnp.transpose(partner, (1, 0)),
    )
    result = pl.pallas_call(
        finish,
        out_shape=jax.ShapeDtypeStruct((5, 125, 2, LANES), F32),
        in_specs=[outside],
        out_specs=outside,
        scratch_shapes=[
            pltpu.VMEM((INST, HALF, LANES), F32),
            pltpu.VMEM((2, ROWS, LANES), F32),
            dma((4,)),
            dma((4,)),
        ],
        compiler_params=pltpu.CompilerParams(vmem_limit_bytes=67_043_328),
    )(parts)
    return jnp.transpose(result, (2, 0, 1, 3))


def solution(mesh):
    placed = (P("inst", None, None, "elem"), P(), P(), P(), P(), P(), P("elem"), P(None, "elem"))
    return jax.shard_map(
        per_device,
        mesh=mesh,
        in_specs=placed,
        out_specs=P("inst", None, None, "elem"),
        check_vma=False,
    )
```

time: 68.9 us -> 66.4 us (0.964)
  Pallas kernels: 67.6 us -> 65.6 us
    pallas_call x1, Pallas kernels: 65.1 us -> 63.2 us  [per_device(): pl.pallas_call(kernel, out_shape=jax.ShapeDtypeStruct((INST, HALF, LANES)...]
where the time goes in v2:
time: 66.4 us; the launch traced here: 66.3 us
  Pallas kernels  65.6 us (99%)
    pallas_call x1, Pallas kernels, per_device(): pl.pallas_call(kernel, out_shape=jax.ShapeDtypeStruct((INST, HALF, LANES)...  63.2 us
    pallas_call x1, Pallas kernels, per_device(): pl.pallas_call(finish, out_shape=jax.ShapeDtypeStruct((5, 125, 2, LANES),...  2.43 us

profile of v2, /device:TPU:1, one launch (start us, length us, event | category | flops | bytes accessed | tf_op | source)
XLA Modules:
  0.0 66.3 jit_solution(6785543174706850024)
XLA Ops:
  0.7 63.2 %shard_map.82.parts_hbm = f32[4,320,128]{2,1,0:T(8,128)} custom-call(f32[5,125,2,128]{3,2,1,0:T(2,128)} %bitcast.9, f32[5,3,5]{2,1,0:T(4,128)} %bitcast.12, f32[3,125,125]{2,1,0:T(8,128)} %derivative_hbm.1, f32[5,6,5]{2,1,0:T(8,128)} %bitcast.11, f32[6,25,125]{2,1,0:T(8,128)} %bitcast.10, f32[1,1]{1,0:T(1,128)} %bitcast.8.frequency_hbm, f32[1,128]{1,0:T(1,128)} %bitcast.14, ...), custom_call_target="tpu_custom_call" | custom-call | tf_op jit(solution)/shard_map/pallas_call | solution.py:552
  63.8 2.4 %shard_map.83 = f32[5,125,2,128]{3,2,1,0:T(2,128)} custom-call(f32[4,320,128]{2,1,0:T(8,128)} %shard_map.82.parts_hbm), custom_call_target="tpu_custom_call" | custom-call | tf_op jit(solution)/shard_map/pallas_call | solution.py:622

commit v3 on v2

--- a/solution.py
+++ b/solution.py
@@ -357,7 +357,21 @@
         target[256 + start : 256 + start + 128, :] = rest
         target[512 + start : 512 + start + 128, :] = fine
 
+    def give_back(targets, remote):
+        for target, away in zip(targets, remote):
+            side = lax.div(target, 2)
+            turn = 64 * lax.rem(target, 2)
+            for start in range(0, HALF, chunk):
+                upper = pltpu.roll(u_ref[side, start : start + chunk, :], turn, 1)
+                lower = pltpu.roll(u_ref[side, HALF + start : HALF + start + chunk, :], 64 - turn, 1)
+                b_send[target, start : start + chunk, :] = jnp.where(lane < 64, upper, lower)
+            if away:
+                exchange(b_send, out_ref, bs_sem, br_sem, target).start()
+            else:
+                pltpu.make_async_copy(b_send.at[target], out_ref.at[target], own_sem).start()
+
     def stage(k, carry):
+        leading = jnp.where(k == STAGES - 1, far, near)
         weight = section_weight(k)
         last = section_weight(k - 1)
         scale = weight * step_lane
@@ -440,7 +454,7 @@
                 interior_traces(side)
                 slide(k + 1, side)
 
-        for side in (near, far):
+        for order, side in enumerate((leading, 1 - leading)):
             all_of(hbuf.at[k, side, pl.ds(0, RING - 1)], hr_sem.at[k, side])
             seen = pick(hbuf, k, side, 1)
 
@@ -460,22 +474,18 @@
             @pl.when(k < STAGES - 1)
             def _(side=side):
                 send_traces(k + 1, side)
+
+            @pl.when(k == STAGES - 1)
+            def _(order=order):
+                if order == 0:
+                    give_back(peers[:2], (True, True))
+                else:
+                    give_back(peers[2:], (True, False))
         return carry
 
     lax.fori_loop(0, STAGES, stage, 0)
 
-    for order, target in enumerate(peers):
-        side = lax.div(target, 2)
-        turn = 64 * lax.rem(target, 2)
-        for start in range(0, HALF, chunk):
-            upper = pltpu.roll(u_ref[side, start : start + chunk, :], turn, 1)
-            lower = pltpu.roll(u_ref[side, HALF + start : HALF + start + chunk, :], 64 - turn, 1)
-            packed = jnp.where(lane < 64, upper, lower)
-            b_send[target, start : start + chunk, :] = packed
-        if order < INST - 1:
-            exchange(b_send, out_ref, bs_sem, br_sem, target).start()
     own = pltpu.make_async_copy(b_send.at[inst], out_ref.at[inst], own_sem)
-    own.start()
     all_of(a_send.at[pl.ds(0, INST - 1)], as_sem)
     all_of(b_send.at[pl.ds(0, INST - 1)], bs_sem)
     all_of(zbuf.at[:, :, pl.ds(0, RING - 1)], zs_sem)

time: 66.4 us -> 65.9 us (level)
  no operation moved by 1% of the time
where the time goes in v3:
time: 65.9 us; the launch traced here: 65.8 us
  Pallas kernels  65.2 us (99%)
  between operations  0.66 us (1%)
    pallas_call x1, Pallas kernels, per_device(): pl.pallas_call(kernel, out_shape=jax.ShapeDtypeStruct((INST, HALF, LANES)...  62.7 us
    pallas_call x1, Pallas kernels, per_device(): pl.pallas_call(finish, out_shape=jax.ShapeDtypeStruct((5, 125, 2, LANES),...  2.43 us

profile of v3, /device:TPU:1, one launch (start us, length us, event | category | flops | bytes accessed | tf_op | source)
XLA Modules:
  0.0 65.8 jit_solution(16778794163815051545)
XLA Ops:
  0.7 62.7 %shard_map.82.parts_hbm = f32[4,320,128]{2,1,0:T(8,128)} custom-call(f32[5,125,2,128]{3,2,1,0:T(2,128)} %bitcast.9, f32[5,3,5]{2,1,0:T(4,128)} %bitcast.12, f32[3,125,125]{2,1,0:T(8,128)} %derivative_hbm.1, f32[5,6,5]{2,1,0:T(8,128)} %bitcast.11, f32[6,25,125]{2,1,0:T(8,128)} %bitcast.10, f32[1,1]{1,0:T(1,128)} %bitcast.8.frequency_hbm, f32[1,128]{1,0:T(1,128)} %bitcast.14, ...), custom_call_target="tpu_custom_call" | custom-call | tf_op jit(solution)/shard_map/pallas_call | solution.py:562
  63.4 2.4 %shard_map.83 = f32[5,125,2,128]{3,2,1,0:T(2,128)} custom-call(f32[4,320,128]{2,1,0:T(8,128)} %shard_map.82.parts_hbm), custom_call_target="tpu_custom_call" | custom-call | tf_op jit(solution)/shard_map/pallas_call | solution.py:632
